TPU v7x, 32 devices: a whole 2x2x4 slice. The times are simulated.
32 devices in a mesh: dp: 8 (over z, y), tensor: 4 (over x, core).
Axes of the slice: x: 2, y: 2, z: 4, core: 2. Of those that a mesh axis runs over, the one named last changes fastest.
Arguments:
- hidden: bfloat16 [128, 4608], P('dp'), may hold values from -6 to 6
- tied_table: bfloat16 [16384, 4608], P(('dp', 'tensor')), may hold values from -0.25 to 0.25
- targets: int32 [128], P('dp'), may hold values from 0 to 16383
- loss_weight: bfloat16 [128], P('dp'), may hold values from 2 to 20
- inputs: int32 [128], P('dp'), may hold values from 0 to 16383
- embed_grad: bfloat16 [128, 4608], P('dp'), may hold values from -0.09375 to 0.09375
Outputs:
- table_grad: bfloat16 [16384, 4608], P(('dp', 'tensor'))
- hidden_grad: float32 [128, 4608], P('dp', 'tensor')
All inputs are finite; a program needn't handle non-finite values.
Results may differ from a plain program's by a relative error of at most 0.0052.
Values may be sent and summed in bfloat16 or wider, within the bound.
A program may use at most 64 MiB of HBM per device.

v0:
```python
import math

import jax
import jax.numpy as jnp
from jax import lax
from jax.sharding import PartitionSpec as P


def squashed(hidden_rows, tied_table):
    logits = lax.dot_general(
        hidden_rows, tied_table, (((1,), (1,)), ((), ())), preferred_element_type=jnp.float32
    )
    return jnp.tanh(logits / 30.0)


def per_device(hidden, tied_table, targets, loss_weight, inputs, embed_grad):
    width = hidden.shape[1]
    vocab_rows = tied_table.shape[0]
    hidden_all, grad_all, target_all, weight_all, input_all = (
        lax.all_gather(hidden, "dp", axis=0, tiled=True),
        lax.all_gather(embed_grad, "dp", axis=0, tiled=True),
        lax.all_gather(targets, "dp", axis=0, tiled=True),
        lax.all_gather(loss_weight, "dp", axis=0, tiled=True),
        lax.all_gather(inputs, "dp", axis=0, tiled=True),
    )
    offset = lax.axis_index(("dp", "tensor")) * vocab_rows
    columns = offset + jnp.arange(vocab_rows)
    squash = squashed(hidden_all, tied_table)
    expo = jnp.exp(30.0 * squash)
    total = lax.psum(jnp.sum(expo, axis=1), ("dp", "tensor"))
    hits = (target_all[:, None] == columns[None, :]).astype(jnp.float32)
    weights = weight_all.astype(jnp.float32)
    dlogit = (weights[:, None] * (expo / total[:, None] - hits) * (1.0 - squash * squash)).astype(
        jnp.bfloat16
    )
    group_rows = lax.psum_scatter(
        jnp.dot(dlogit, tied_table, preferred_element_type=jnp.float32),
        "dp",
        scatter_dimension=0,
        tiled=True,
    )
    hidden_grad = lax.psum_scatter(group_rows, "tensor", scatter_dimension=1, tiled=True)
    head_term = lax.dot_general(
        dlogit, hidden_all, (((0,), (0,)), ((), ())), preferred_element_type=jnp.float32
    )
    onehot = (input_all[None, :] == columns[:, None]).astype(jnp.bfloat16)
    embed_term = jnp.dot(onehot, grad_all, preferred_element_type=jnp.float32)
    table_grad = (head_term + math.sqrt(width) * embed_term).astype(jnp.bfloat16)
    return (table_grad, hidden_grad)


def solution(mesh):
    placed = (P("dp", None), P(("dp", "tensor"), None), P("dp"), P("dp"), P("dp"), P("dp", None))
    return jax.shard_map(
        per_device,
        mesh=mesh,
        in_specs=placed,
        out_specs=(P(("dp", "tensor"), None), P("dp", "tensor")),
        check_vma=False,
    )
```

profile of v0, /device:TPU:0, one launch (start us, length us, event | category | flops | bytes accessed | tf_op | source)
XLA Modules:
  0.0 241.8 jit_solution(12632579317556245795)
XLA Ops:
  7.2 0.0 all-gather.3.cloned.1.call-start
  7.2 0.7 all-gather.3.cloned.1.call-update
  7.9 0.0 reduce-scatter.3.cloned.1.call-start
  8.0 1.2 dynamic-slice
  9.9 0.9 dynamic-update-slice
  10.7 23.2 %all-reduce = bf16[128]{0:T(256)(128)(2,1)S(1)} all-reduce(bf16[128]{0:T(256)(128)(2,1)S(1)} %dynamic-update-slice), channel_id=1, replica_groups=mesh['dp'=8,'tensor'=4] {'dp'}, use_global_device_ids=true, to_apply=%add | all-reduce | flops 128 | bytes 512
  34.0 0.9 dynamic-update-slice.1
  34.8 0.8 dynamic-update-slice.2
  35.7 6.8 %all-reduce.3 = (s32[128]{0:T(128)S(1)}, s32[128]{0:T(128)S(1)}) all-reduce(s32[128]{0:T(128)S(1)} %dynamic-update-slice.1, s32[128]{0:T(128)S(1)} %dynamic-update-slice.2), channel_id=1, replica_groups=mesh['dp'=8,'tensor'=4] {'dp'}, use_global_device_ids=true, to_apply=%add.1 | all-reduce | flops 256 | bytes 2048
  42.5 11.3 %all-gather.3.cloned.1.call-done = bf16[128,4608]{1,0:T(8,128)(2,1)} async-done(((bf16[16,4608]{1,0:T(8,128)(2,1)}), bf16[128,4608]{1,0:T(8,128)(2,1)}) %all-gather.3.cloned.1.call-update) | async-done | bytes 1179664 | tf_op jit(solution)/shard_map/all_gather | solution.py:20
  53.8 4.4 %fusion.1 = (f32[128]{0:T(128)S(1)}, f32[128,512]{1,0:T(8,128)S(1)}) fusion(bf16[128,4608]{1,0:T(8,128)(2,1)} %all-gather.3.cloned.1.call-done, bf16[512,4608]{1,0:T(8,128)(2,1)} %param.7), kind=kOutput, calls=%fused_computation.5 | convolution fusion | flops 604176256 | bytes 6160896 | tf_op jit(solution)/shard_map/dot_general | solution.py:10
  58.3 38.7 %psum.7 = f32[128]{0:T(128)S(1)} all-reduce(f32[128]{0:T(128)S(1)} %get-tuple-element.4), channel_id=1, replica_groups=mesh['dp'=8,'tensor'=4] {'dp','tensor'}, use_global_device_ids=true, to_apply=%region_1.0 | all-reduce | flops 128 | bytes 1024 | tf_op jit(solution)/shard_map/psum | solution.py:30
  96.9 0.0 copy-start
  96.9 4.7 %fusion.5 = f32[128,4608]{1,0:T(8,128)} fusion(bf16[512,4608]{1,0:T(8,128)(2,1)} %param.7, f32[128,512]{1,0:T(8,128)S(1)} %get-tuple-element.5, s32[512]{0:T(512)S(1)} %iota_add_fusion, f32[128]{0:T(128)S(1)} %psum.7, f32[128]{0:T(128)S(1)} %convert_element_type.13, s32[128]{0:T(128)S(1)} %get-tuple-element.2), kind=kOutput, calls=%fused_computation.10 | convolution fusion | flops 604635136 | bytes 7343616 | tf_op jit(solution)/shard_map/dot_general | solution.py:37
  101.6 0.0 reduce-scatter.3.cloned.1.call-update
  101.7 0.0 all-gather.5.cloned.1.call-start
  101.7 0.7 all-gather.5.cloned.1.call-update
  102.4 0.0 reduce-scatter.5.cloned.1.call-start
  102.5 0.0 copy-done
  102.5 5.2 %fusion.6 = f32[512,4608]{1,0:T(8,128)} fusion(bf16[128,4608]{1,0:T(8,128)(2,1)S(1)} %copy-done, f32[128,512]{1,0:T(8,128)S(1)} %get-tuple-element.5, s32[512]{0:T(512)S(1)} %iota_add_fusion, f32[128]{0:T(128)S(1)} %psum.7, f32[128]{0:T(128)S(1)} %convert_element_type.13, s32[128]{0:T(128)S(1)} %get-tuple-element.2), kind=kOutput, calls=%fused_computation.11 | convolution fusion | flops 604635136 | bytes 10882560 | tf_op jit(solution)/shard_map/dot_general | solution.py:43
  107.6 63.3 %reduce-scatter.3.cloned.1.call-done = f32[16,4608]{1,0:T(8,128)} async-done(((f32[128,4608]{1,0:T(8,128)}), f32[16,4608]{1,0:T(8,128)}) %reduce-scatter.3.cloned.1.call-update) | async-done | bytes 294928 | tf_op jit(solution)/shard_map/reduce_scatter | solution.py:36
  171.0 0.0 reduce-scatter.5.cloned.1.call-update
  171.0 42.3 %all-gather.5.cloned.1.call-done = bf16[128,4608]{1,0:T(8,128)(2,1)} async-done(((bf16[16,4608]{1,0:T(8,128)(2,1)}), bf16[128,4608]{1,0:T(8,128)(2,1)}) %all-gather.5.cloned.1.call-update) | async-done | bytes 1179664 | tf_op jit(solution)/shard_map/all_gather | solution.py:21
  213.3 7.7 %add_convert_fusion = bf16[512,4608]{1,0:T(8,128)(2,1)} fusion(f32[512,4608]{1,0:T(8,128)} %fusion.6, bf16[128,4608]{1,0:T(8,128)(2,1)} %all-gather.5.cloned.1.call-done, s32[128]{0:T(128)S(1)} %get-tuple-element.3, s32[512]{0:T(512)S(1)} %iota_add_fusion), kind=kOutput, calls=%fused_computation | convolution fusion | flops 611123200 | bytes 15337984 | tf_op jit(solution)/shard_map/dot_general | solution.py:47
  220.9 14.3 %reduce-scatter.5.cloned.1.call-done = f32[16,1152]{1,0:T(8,128)} async-done(((f32[16,4608]{1,0:T(8,128)}), f32[16,1152]{1,0:T(8,128)}) %reduce-scatter.5.cloned.1.call-update) | async-done | bytes 73744 | tf_op jit(solution)/shard_map/reduce_scatter | solution.py:42
  (5 shorter events, 0.0 us)
Async XLA Ops:
  7.2 46.7 %all-gather.3.cloned.1.call-start = ((), (), s32[]{:S(2)}) async-start(), calls=%async_computation.2 | async-start | bytes 1327104 | tf_op jit(solution)/shard_map/all_gather | solution.py:20
  7.9 163.1 %reduce-scatter.3.cloned.1.call-start = ((), (), s32[]{:S(2)}) async-start(), calls=%async_computation.4 | async-start | bytes 2654208 | tf_op jit(solution)/shard_map/reduce_scatter | solution.py:36
  96.9 5.5 %copy-start = (bf16[128,4608]{1,0:T(8,128)(2,1)S(1)}, bf16[128,4608]{1,0:T(8,128)(2,1)}, u32[]{:S(2)}) copy-start(bf16[128,4608]{1,0:T(8,128)(2,1)} %all-gather.3.cloned.1.call-done) | copy-start | bytes 3538948
  101.7 111.6 %all-gather.5.cloned.1.call-start = ((), (), s32[]{:S(2)}) async-start(), calls=%async_computation.3 | async-start | bytes 1327104 | tf_op jit(solution)/shard_map/all_gather | solution.py:21
  102.4 132.9 %reduce-scatter.5.cloned.1.call-start = ((), (), s32[]{:S(2)}) async-start(), calls=%async_computation.5 | async-start | bytes 368640 | tf_op jit(solution)/shard_map/reduce_scatter | solution.py:42
Sparse Core Ops, SparseCore 0:
  10.2 43.6 all-gather.2
  101.8 69.1 reduce-scatter.2
  173.1 40.0 all-gather.4
  216.2 19.0 reduce-scatter.4
where the time goes:
time: 242 us
  waiting for transfers between devices  133 us (55%)
  blocking collectives  68.7 us (28%)
  matrix products  22 us (9%)
  between operations  14.5 us (6%)
  local copies, waits for them, and re-layouts  3.81 us (2%)
    reduce_scatter x1, waiting for transfers between devices, per_device(): lax.psum_scatter(jnp.dot(dlogit, tied_table, preferred_element_type=jnp.f...  63.3 us
    all_gather x1, waiting for transfers between devices, per_device(): lax.all_gather(embed_grad, 'dp', axis=0, tiled=True)  42.3 us
    psum x1, blocking collectives, per_device(): total = lax.psum(jnp.sum(expo, axis=1), ('dp', 'tensor'))  38.7 us
    unnamed x2, blocking collectives  30.1 us
    reduce_scatter x1, waiting for transfers between devices, per_device(): lax.psum_scatter(group_rows, 'tensor', scatter_dimension=1, tiled=True)  14.3 us
    all_gather x1, waiting for transfers between devices, per_device(): lax.all_gather(hidden, 'dp', axis=0, tiled=True)  11.3 us
    dot_general x1, matrix products, per_device(): embed_term = jnp.dot(onehot, grad_all, preferred_element_type=jnp.float32)  7.67 us
    dot_general x1, matrix products, per_device(): lax.dot_general(dlogit, hidden_all, (((0,), (0,)), ((), ())), preferred_e...  5.16 us
  transfers between devices with their start and end apart: 4, of which 4 were waited for; matrix products, arithmetic and copies ran while one was open for 7% of the time, Pallas kernels for 0%

commit v1 on v0

v1 whole, which is shorter than its diff:
```python
import functools
import math

import jax
import jax.numpy as jnp
from jax import lax
from jax.experimental import pallas as pl
from jax.experimental.pallas import tpu as pltpu
from jax.sharding import PartitionSpec as P

MESH = pl.DeviceIdType.MESH
ROWS = (((0,), (0,)), ((), ()))
LANES = (((1,), (1,)), ((), ()))


def kernel(
    n_dp, n_t, scale,
    hid, emb, meta, table, tg, hg,
    ha, ea, ma, tab, tgb, sq, dl, oh, dlt, sa, sd, pf, pb, r1, qb, r2, gb, r3,
    h_z, h_y, h_s, h_r, h_r2, e_z, e_y, e_s, e_r, e_r2, m_z, m_y, m_r,
    sa_s, sa_r, sd_s, sd_r, a_s, a_r, b_s, b_r, c_s, c_r, tab_s, tg_s,
):
    d, t = lax.axis_index("dp"), lax.axis_index("tensor")
    n_a, n_x = n_dp // 2, n_t // 2
    a, b = lax.div(d, 2), lax.rem(d, 2)
    x, c = lax.div(t, 2), lax.rem(t, 2)
    side, sib = a * 2 + 1 - b, x * 2 + 1 - c
    rows, width = hid.shape
    half = width // 2
    tokens = n_dp * rows
    vocab = tab.shape[0]
    cols = width // n_t

    load = pltpu.make_async_copy(table, tab, tab_s)
    load.start()
    for h in range(2):
        ha[h, d] = hid[:, h * half:(h + 1) * half]
        ea[h, d] = emb[:, h * half:(h + 1) * half]
    ma[d] = meta[...]

    barrier = pltpu.get_barrier_semaphore()
    for j in range(1, n_t):
        pl.semaphore_signal(barrier, inc=1, device_id=(d, lax.rem(t + j, n_t)), device_id_type=MESH)
    for j in range(1, n_dp):
        pl.semaphore_signal(barrier, inc=1, device_id=(lax.rem(d + j, n_dp), t), device_id_type=MESH)
    pl.semaphore_wait(barrier, n_t + n_dp - 2)

    sent = []

    def send(ref, dst, ss, rs, dev):
        copy = pltpu.make_async_remote_copy(
            src_ref=ref, dst_ref=dst, send_sem=ss, recv_sem=rs, device_id=dev, device_id_type=MESH
        )
        copy.start()
        sent.append(copy)

    def arrived(ref, ss, rs):
        pltpu.make_async_remote_copy(
            src_ref=ref, dst_ref=ref, send_sem=ss, recv_sem=rs, device_id=(side, t), device_id_type=MESH
        ).wait_recv()

    def up(j):
        return lax.rem(a + j, n_a) * 2 + b

    def down(j):
        return lax.rem(a + n_a - j, n_a) * 2

    def gather_start(buf, z, y, r):
        for j in range(1, n_a):
            send(buf.at[c, d], buf.at[c, d], z.at[j], r.at[d], (up(j), t))
        send(buf.at[c, d], buf.at[c, d], y.at[0], r.at[d], (side, t))

    def gather_far(buf, z, y, s, r, r2):
        for j in range(1, n_a):
            k = down(j) + b
            arrived(buf.at[c, k], z.at[j], r.at[k])
            send(buf.at[c, k], buf.at[c, k], y.at[j], r.at[k], (side, t))
            send(buf.at[c, k], buf.at[c, k], s.at[k], r2.at[k], (d, sib))

    def gather_side(buf, z, s, r, r2):
        for j in range(n_a):
            k = down(j) + 1 - b
            arrived(buf.at[c, k], z.at[0], r.at[k])
            send(buf.at[c, k], buf.at[c, k], s.at[k], r2.at[k], (d, sib))

    def gather_end(buf, z, r2):
        for j in range(1, n_dp):
            k = lax.rem(d + j, n_dp)
            arrived(buf.at[1 - c, k], z.at[0], r2.at[k])

    for j in range(1, n_a):
        send(ma.at[d], ma.at[d], m_z.at[j], m_r.at[d], (up(j), t))
    send(ma.at[d], ma.at[d], m_y.at[0], m_r.at[d], (side, t))
    gather_start(ha, h_z, h_y, h_r)
    gather_far(ha, h_z, h_y, h_s, h_r, h_r2)
    for j in range(1, n_a):
        k = down(j) + b
        arrived(ma.at[k], m_z.at[0], m_r.at[k])
        send(ma.at[k], ma.at[k], m_y.at[j], m_r.at[k], (side, t))
    gather_side(ha, h_z, h_s, h_r, h_r2)
    gather_start(ea, e_z, e_y, e_r)
    gather_end(ha, h_z, h_r2)
    load.wait()

    piece = min(vocab, 256)
    left = ha[0].reshape(tokens, half)
    right = ha[1].reshape(tokens, half)

    def logit_rows(i, acc):
        at = pl.ds(pl.multiple_of(i * piece, piece), piece)
        logits = lax.dot_general(tab[at, :half], left, LANES, preferred_element_type=jnp.float32)
        logits += lax.dot_general(tab[at, half:], right, LANES, preferred_element_type=jnp.float32)
        squash = jnp.tanh(logits / 30.0)
        sq[at, :] = squash
        return acc + jnp.sum(jnp.exp(30.0 * squash), axis=0, keepdims=True)

    part = lax.fori_loop(0, vocab // piece, logit_rows, jnp.zeros((1, tokens), jnp.float32))
    sa[t] = jnp.broadcast_to(part, (8, tokens))
    for j in range(1, n_t):
        send(sa.at[t], sa.at[t], sa_s.at[j], sa_r.at[t], (d, lax.rem(t + j, n_t)))
    for j in range(1, n_a):
        k = down(j) + 1 - b
        arrived(ma.at[k], m_z.at[0], m_r.at[k])
    arrived(ma.at[side], m_z.at[0], m_r.at[side])
    for j in range(1, n_t):
        k = lax.rem(t + j, n_t)
        arrived(sa.at[k], sa_s.at[0], sa_r.at[k])
    sd[d] = jnp.sum(sa[...], axis=0)
    for j in range(1, n_dp):
        send(sd.at[d], sd.at[d], sd_s.at[j], sd_r.at[d], (lax.rem(d + j, n_dp), t))
    gather_far(ea, e_z, e_y, e_s, e_r, e_r2)
    ids = jnp.transpose(ma[...].reshape(tokens, 128))
    base = (d * n_t + t) * vocab
    column = (base + lax.broadcasted_iota(jnp.int32, (vocab, tokens), 0)).astype(jnp.float32)
    oh[...] = jnp.where(column == ids[1:2, :], 1.0, 0.0).astype(jnp.bfloat16)
    for j in range(1, n_dp):
        k = lax.rem(d + j, n_dp)
        arrived(sd.at[k], sd_s.at[0], sd_r.at[k])
    total = jnp.sum(sd[...], axis=0)[0:1, :]
    squash = sq[...]
    hits = jnp.where(column == ids[0:1, :], 1.0, 0.0)
    dlogit = ids[2:3, :] * (jnp.exp(30.0 * squash) / total - hits) * (1.0 - squash * squash)
    dl[...] = dlogit.astype(jnp.bfloat16)
    dlt[...] = jnp.transpose(dlogit).astype(jnp.bfloat16)

    for u in range(n_x):
        for v in range(2):
            k = 2 * u + v
            term = jnp.dot(
                dlt[...], tab[:, k * cols:(k + 1) * cols], preferred_element_type=jnp.float32
            )
            pf[k] = term
            pb[k] = term.astype(jnp.bfloat16)
        send(pb.at[2 * u + 1 - c], r1.at[u], a_s.at[u], a_r.at[u], (d, sib))
    for j in list(range(1, n_x)) + [0]:
        u = lax.rem(x + j, n_x)
        arrived(r1.at[u], a_s.at[0], a_r.at[u])
        pair = pf[2 * u + c] + r1[u].astype(jnp.float32)
        if j:
            qb[u] = pair.astype(jnp.bfloat16)
            send(qb.at[u], r2.at[x], b_s.at[j], b_r.at[x], (d, u * 2 + c))
        else:
            pf[2 * u + c] = pair
    gather_side(ea, e_z, e_s, e_r, e_r2)
    gather_end(ea, e_z, e_r2)

    step = 256
    stores = []

    def table_half(h):
        def table_cols(i, carry):
            at = pl.ds(pl.multiple_of(i * step, step), step)
            head = jnp.dot(
                dl[...], ha[h, :, :, at].reshape(tokens, step), preferred_element_type=jnp.float32
            )
            tail = jnp.dot(
                oh[...], ea[h, :, :, at].reshape(tokens, step), preferred_element_type=jnp.float32
            )
            tgb[h, :, at] = (head + scale * tail).astype(jnp.bfloat16)
            return carry

        lax.fori_loop(0, half // step, table_cols, 0)
        copy = pltpu.make_async_copy(tgb.at[h], tg.at[:, h * half:(h + 1) * half], tg_s.at[h])
        copy.start()
        stores.append(copy)

    table_half(0)
    mine = pf[2 * x + c]
    for j in range(1, n_x):
        u = lax.rem(x + j, n_x)
        arrived(r2.at[u], b_s.at[0], b_r.at[u])
        mine = mine + r2[u].astype(jnp.float32)
    pf[2 * x + c] = mine
    gb[...] = mine.reshape(n_dp, rows, cols).astype(jnp.bfloat16)
    for j in range(1, n_dp):
        k = lax.rem(d + j, n_dp)
        send(gb.at[k], r3.at[d], c_s.at[j], c_r.at[d], (k, t))
    table_half(1)
    out = pf[2 * x + c, pl.ds(pl.multiple_of(d * rows, rows), rows), :]
    for j in range(1, n_dp):
        k = lax.rem(d + j, n_dp)
        arrived(r3.at[k], c_s.at[0], c_r.at[k])
        out = out + r3[k].astype(jnp.float32)
    hg[...] = out
    for copy in sent:
        copy.wait_send()
    for copy in stores:
        copy.wait()


def per_device(n_dp, n_t, hidden, tied_table, targets, loss_weight, inputs, embed_grad):
    rows, width = hidden.shape
    vocab = tied_table.shape[0]
    tokens, half, cols, n_x = n_dp * rows, width // 2, width // n_t, n_t // 2
    f32, bf16 = jnp.float32, jnp.bfloat16
    lane = lax.broadcasted_iota(jnp.int32, (rows, 128), 1)
    meta = jnp.where(
        lane == 0,
        targets.astype(f32)[:, None],
        jnp.where(lane == 1, inputs.astype(f32)[:, None], loss_weight.astype(f32)[:, None]),
    )
    vmem = pl.BlockSpec(memory_space=pltpu.VMEM)
    dma = lambda n: pltpu.SemaphoreType.DMA((n,))
    n_a = n_dp // 2
    gather_sems = [dma(n_a), dma(n_a), dma(n_dp), dma(n_dp), dma(n_dp)]
    return pl.pallas_call(
        functools.partial(kernel, n_dp, n_t, math.sqrt(width)),
        out_shape=(
            jax.ShapeDtypeStruct((vocab, width), bf16),
            jax.ShapeDtypeStruct((rows, cols), f32),
        ),
        in_specs=[vmem, vmem, vmem, pl.BlockSpec(memory_space=pl.ANY)],
        out_specs=(pl.BlockSpec(memory_space=pl.ANY), vmem),
        scratch_shapes=[
            pltpu.VMEM((2, n_dp, rows, half), bf16),
            pltpu.VMEM((2, n_dp, rows, half), bf16),
            pltpu.VMEM((n_dp, rows, 128), f32),
            pltpu.VMEM((vocab, width), bf16),
            pltpu.VMEM((2, vocab, half), bf16),
            pltpu.VMEM((vocab, tokens), f32),
            pltpu.VMEM((vocab, tokens), bf16),
            pltpu.VMEM((vocab, tokens), bf16),
            pltpu.VMEM((tokens, vocab), bf16),
            pltpu.VMEM((n_t, 8, tokens), f32),
            pltpu.VMEM((n_dp, 8, tokens), f32),
            pltpu.VMEM((n_t, tokens, cols), f32),
            pltpu.VMEM((n_t, tokens, cols), bf16),
            pltpu.VMEM((n_x, tokens, cols), bf16),
            pltpu.VMEM((n_x, tokens, cols), bf16),
            pltpu.VMEM((n_x, tokens, cols), bf16),
            pltpu.VMEM((n_dp, rows, cols), bf16),
            pltpu.VMEM((n_dp, rows, cols), bf16),
            *gather_sems, *gather_sems,
            dma(n_a), dma(n_a), dma(n_dp),
            dma(n_t), dma(n_t), dma(n_dp), dma(n_dp),
            dma(n_x), dma(n_x), dma(n_x), dma(n_x), dma(n_dp), dma(n_dp),
            pltpu.SemaphoreType.DMA, dma(2),
        ],
        compiler_params=pltpu.CompilerParams(
            collective_id=0, has_side_effects=True, vmem_limit_bytes=56 << 20
        ),
    )(hidden, embed_grad, meta, tied_table)


def solution(mesh):
    placed = (P("dp", None), P(("dp", "tensor"), None), P("dp"), P("dp"), P("dp"), P("dp", None))
    return jax.shard_map(
        functools.partial(per_device, mesh.shape["dp"], mesh.shape["tensor"]),
        mesh=mesh,
        in_specs=placed,
        out_specs=(P(("dp", "tensor"), None), P("dp", "tensor")),
        check_vma=False,
    )
```

time: 242 us -> 55.8 us (0.23)
  waiting for transfers between devices: 133 us -> 0 us
  blocking collectives: 68.7 us -> 0 us
  Pallas kernels: 0 us -> 46.8 us
  matrix products: 22 us -> 0 us
  between operations: 14.5 us -> 0.65 us
  other arithmetic: 0.01 us -> 2.65 us
    reduce_scatter x2 -> x0, waiting for transfers between devices: 77.7 us -> none  [the longest x1 63.3 us: per_device(): lax.psum_scatter(jnp.dot(dlogit, tied_table, preferred_element_type=jnp.f...]
    all_gather x2 -> x0, waiting for transfers between devices: 53.6 us -> none  [the longest x1 42.3 us: per_device(): lax.all_gather(embed_grad, 'dp', axis=0, tiled=True)]
    pallas_call x0 -> x1, Pallas kernels: none -> 46.8 us  [per_device(): pl.pallas_call(functools.partial(kernel, n_dp, n_t, math.sqrt(width)), ou...]
    psum x1 -> x0, blocking collectives: 38.7 us -> none  [per_device(): total = lax.psum(jnp.sum(expo, axis=1), ('dp', 'tensor'))]
    unnamed x2 -> x0, blocking collectives: 30.1 us -> none
    dot_general x4 -> x0, matrix products: 22 us -> none  [the longest x1 7.67 us: per_device(): embed_term = jnp.dot(onehot, grad_all, preferred_element_type=jnp.float32)]
    unnamed x9 -> x4, local copies, waits for them, and re-layouts: 3.81 us -> 5.49 us
  transfers between devices with their start and end apart: 4 -> 0, of which waited for: 4 -> 0; matrix products, arithmetic and copies ran while one was open for 7% -> 0% of each run, Pallas kernels for 0% -> 0%
where the time goes in v1:
time: 55.8 us; the launch traced here: 55.6 us
  Pallas kernels  46.8 us (84%)
  local copies, waits for them, and re-layouts  5.49 us (10%)
  other arithmetic  2.65 us (5%)
  between operations  0.65 us (1%)
    pallas_call x1, Pallas kernels, per_device(): pl.pallas_call(functools.partial(kernel, n_dp, n_t, math.sqrt(width)), ou...  46.8 us
    unnamed x4, local copies, waits for them, and re-layouts  5.49 us

profile of v1, /device:TPU:0, one launch (start us, length us, event | category | flops | bytes accessed | tf_op | source)
XLA Modules:
  0.0 55.6 jit_solution(7429280074012738502)
XLA Ops:
  0.6 0.7 %convert_element_type.9 = f32[16]{0:T(128)S(1)} convert(s32[16]{0:T(128)} %param.8) | non-fusion elementwise | flops 16 | bytes 128 | tf_op jit(solution)/shard_map/convert_element_type | solution.py:219
  1.3 0.7 %convert_element_type.11 = f32[16]{0:T(128)S(1)} convert(bf16[16]{0:T(256)(128)(2,1)} %param.9) | non-fusion elementwise | flops 16 | bytes 96 | tf_op jit(solution)/shard_map/convert_element_type | solution.py:220
  1.9 0.7 %convert_element_type.10 = f32[16]{0:T(128)S(1)} convert(s32[16]{0:T(128)} %param.10) | non-fusion elementwise | flops 16 | bytes 128 | tf_op jit(solution)/shard_map/convert_element_type | solution.py:220
  2.6 0.7 %select_select_fusion.meta = f32[16,128]{1,0:T(8,128)} fusion(f32[16]{0:T(128)S(1)} %convert_element_type.11, f32[16]{0:T(128)S(1)} %convert_element_type.10, f32[16]{0:T(128)S(1)} %convert_element_type.9, pred[128]{0:T(512)(128)(4,1)S(1)} %get-tuple-element.2, pred[128]{0:T(512)(128)(4,1)S(1)} %get-tuple-element.3), kind=kLoop, calls=%fused_computation | loop fusion | flops 4096 | bytes 8640 | tf_op jit(solution)/shard_map/jit(_where)/select_n | solution.py:217
  3.3 46.8 %shard_map.77 = (bf16[512,4608]{1,0:T(8,128)(2,1)}, f32[16,1152]{1,0:T(8,128)}) custom-call(bf16[16,4608]{1,0:T(8,128)(2,1)} %hid.1, bf16[16,4608]{1,0:T(8,128)(2,1)} %emb.1, f32[16,128]{1,0:T(8,128)} %select_select_fusion.meta, bf16[512,4608]{1,0:T(8,128)(2,1)} %table.1), custom_call_target="tpu_custom_call" | custom-call | tf_op jit(solution)/shard_map/pallas_call | solution.py:226
  50.1 0.0 copy-start
  50.1 4.9 %copy.10 = bf16[512,4608]{1,0:T(8,128)(2,1)} copy(bf16[512,4608]{1,0:T(8,128)(2,1)} %get-tuple-element.6) | data formatting | bytes 9437184
  55.0 0.0 copy-done
  55.0 0.6 %copy.11 = f32[16,1152]{1,0:T(8,128)} copy(f32[16,1152]{1,0:T(8,128)S(1)} %copy-done) | data formatting | bytes 147456
  (1 shorter events, 0.0 us)
Async XLA Ops:
  50.1 4.9 %copy-start = (f32[16,1152]{1,0:T(8,128)S(1)}, f32[16,1152]{1,0:T(8,128)}, u32[]{:S(2)}) copy-start(f32[16,1152]{1,0:T(8,128)} %get-tuple-element.7) | copy-start | bytes 221188

commit v2 on v1

--- a/solution.py
+++ b/solution.py
@@ -15,10 +15,10 @@
 
 def kernel(
     n_dp, n_t, scale,
-    hid, emb, meta, table, tg, hg,
-    ha, ea, ma, tab, tgb, sq, dl, oh, dlt, sa, sd, pf, pb, r1, qb, r2, gb, r3,
+    hid, emb, targets, inputs, weights, table, tg, hg,
+    ha, ea, ma, ids, tab, sq, dl, oh, dlt, sa, sd, terms, pf, pb, r1, qb, r2, gb, r3,
     h_z, h_y, h_s, h_r, h_r2, e_z, e_y, e_s, e_r, e_r2, m_z, m_y, m_r,
-    sa_s, sa_r, sd_s, sd_r, a_s, a_r, b_s, b_r, c_s, c_r, tab_s, tg_s,
+    sa_s, sa_r, sd_s, sd_r, a_s, a_r, b_s, b_r, c_s, c_r, tab_s,
 ):
     d, t = lax.axis_index("dp"), lax.axis_index("tensor")
     n_a, n_x = n_dp // 2, n_t // 2
@@ -36,7 +36,10 @@
     for h in range(2):
         ha[h, d] = hid[:, h * half:(h + 1) * half]
         ea[h, d] = emb[:, h * half:(h + 1) * half]
-    ma[d] = meta[...]
+    ma[d] = jnp.zeros(ma.shape[1:], jnp.float32)
+    ma[d, 0:1, 0:rows] = targets[...].astype(jnp.float32)
+    ma[d, 1:2, 0:rows] = inputs[...].astype(jnp.float32)
+    ma[d, 2:3, 0:rows] = weights[...].astype(jnp.float32)
 
     barrier = pltpu.get_barrier_semaphore()
     for j in range(1, n_t):
@@ -99,22 +102,31 @@
         send(ma.at[k], ma.at[k], m_y.at[j], m_r.at[k], (side, t))
     gather_side(ha, h_z, h_s, h_r, h_r2)
     gather_start(ea, e_z, e_y, e_r)
-    gather_end(ha, h_z, h_r2)
     load.wait()
-
     piece = min(vocab, 256)
-    left = ha[0].reshape(tokens, half)
-    right = ha[1].reshape(tokens, half)
-
-    def logit_rows(i, acc):
+
+    def logits(i, core):
         at = pl.ds(pl.multiple_of(i * piece, piece), piece)
-        logits = lax.dot_general(tab[at, :half], left, LANES, preferred_element_type=jnp.float32)
-        logits += lax.dot_general(tab[at, half:], right, LANES, preferred_element_type=jnp.float32)
-        squash = jnp.tanh(logits / 30.0)
+        side_cols = pl.ds(pl.multiple_of(core * half, half), half)
+        return at, lax.dot_general(
+            tab[at, side_cols], ha[core].reshape(tokens, half), LANES,
+            preferred_element_type=jnp.float32,
+        )
+
+    def first_half(i, carry):
+        at, product = logits(i, c)
+        sq[at, :] = product
+        return carry
+
+    def second_half(i, acc):
+        at, product = logits(i, 1 - c)
+        squash = jnp.tanh((sq[at, :] + product) / 30.0)
         sq[at, :] = squash
         return acc + jnp.sum(jnp.exp(30.0 * squash), axis=0, keepdims=True)
 
-    part = lax.fori_loop(0, vocab // piece, logit_rows, jnp.zeros((1, tokens), jnp.float32))
+    lax.fori_loop(0, vocab // piece, first_half, 0)
+    gather_end(ha, h_z, h_r2)
+    part = lax.fori_loop(0, vocab // piece, second_half, jnp.zeros((1, tokens), jnp.float32))
     sa[t] = jnp.broadcast_to(part, (8, tokens))
     for j in range(1, n_t):
         send(sa.at[t], sa.at[t], sa_s.at[j], sa_r.at[t], (d, lax.rem(t + j, n_t)))
@@ -129,7 +141,8 @@
     for j in range(1, n_dp):
         send(sd.at[d], sd.at[d], sd_s.at[j], sd_r.at[d], (lax.rem(d + j, n_dp), t))
     gather_far(ea, e_z, e_y, e_s, e_r, e_r2)
-    ids = jnp.transpose(ma[...].reshape(tokens, 128))
+    for k in range(n_dp):
+        ids[:, k * rows:(k + 1) * rows] = ma[k, :, 0:rows]
     base = (d * n_t + t) * vocab
     column = (base + lax.broadcasted_iota(jnp.int32, (vocab, tokens), 0)).astype(jnp.float32)
     oh[...] = jnp.where(column == ids[1:2, :], 1.0, 0.0).astype(jnp.bfloat16)
@@ -143,31 +156,59 @@
     dl[...] = dlogit.astype(jnp.bfloat16)
     dlt[...] = jnp.transpose(dlogit).astype(jnp.bfloat16)
 
-    for u in range(n_x):
-        for v in range(2):
-            k = 2 * u + v
-            term = jnp.dot(
-                dlt[...], tab[:, k * cols:(k + 1) * cols], preferred_element_type=jnp.float32
-            )
-            pf[k] = term
-            pb[k] = term.astype(jnp.bfloat16)
-        send(pb.at[2 * u + 1 - c], r1.at[u], a_s.at[u], a_r.at[u], (d, sib))
-    for j in list(range(1, n_x)) + [0]:
+    def term(k):
+        return jnp.dot(dlt[...], tab[:, k], preferred_element_type=jnp.float32)
+
+    def columns(k):
+        return pl.ds(pl.multiple_of(k * cols, 128), cols)
+
+    aligned = cols % 128 == 0
+    if not aligned:
+        for k in range(n_t):
+            terms[k] = term(slice(k * cols, (k + 1) * cols))
+    order = list(range(1, n_x)) + [0]
+    for j in order:
+        u = lax.rem(x + j, n_x)
+        give, keep = 2 * u + 1 - c, 2 * u + c
+        pb[u] = (term(columns(give)) if aligned else terms[give]).astype(jnp.bfloat16)
+        send(pb.at[u], r1.at[u], a_s.at[u], a_r.at[u], (d, sib))
+        pf[u] = term(columns(keep)) if aligned else terms[keep]
+
+    n_q = 2
+    slots = n_dp // n_q
+
+    def pair(u, i):
+        k = lax.rem(d + 1 + i, n_dp)
+        at = pl.ds(pl.multiple_of(k * rows, rows), rows)
+        return pf[u, at, :] + r1[u, at, :].astype(jnp.float32)
+
+    for j in order:
         u = lax.rem(x + j, n_x)
         arrived(r1.at[u], a_s.at[0], a_r.at[u])
-        pair = pf[2 * u + c] + r1[u].astype(jnp.float32)
         if j:
-            qb[u] = pair.astype(jnp.bfloat16)
-            send(qb.at[u], r2.at[x], b_s.at[j], b_r.at[x], (d, u * 2 + c))
-        else:
-            pf[2 * u + c] = pair
+            for q in range(n_q):
+                for i in range(q * slots, (q + 1) * slots):
+                    qb[u, i] = pair(u, i).astype(jnp.bfloat16)
+                span = pl.ds(q * slots, slots)
+                send(qb.at[u, span], r2.at[x, span], b_s.at[j, q], b_r.at[x, q], (d, u * 2 + c))
     gather_side(ea, e_z, e_s, e_r, e_r2)
+    for q in range(n_q):
+        for j in range(1, n_x):
+            u = lax.rem(x + j, n_x)
+            arrived(r2.at[u, pl.ds(q * slots, slots)], b_s.at[0, 0], b_r.at[u, q])
+        for i in range(q * slots, (q + 1) * slots):
+            mine = pair(x, i)
+            for j in range(1, n_x):
+                mine = mine + r2[lax.rem(x + j, n_x), i].astype(jnp.float32)
+            if i < n_dp - 1:
+                gb[i] = mine.astype(jnp.bfloat16)
+                send(gb.at[i], r3.at[d], c_s.at[i], c_r.at[d], (lax.rem(d + 1 + i, n_dp), t))
+            else:
+                hg[...] = mine
     gather_end(ea, e_z, e_r2)
 
     step = 256
-    stores = []
-
-    def table_half(h):
+    for h in range(2):
         def table_cols(i, carry):
             at = pl.ds(pl.multiple_of(i * step, step), step)
             head = jnp.dot(
@@ -176,27 +217,13 @@
             tail = jnp.dot(
                 oh[...], ea[h, :, :, at].reshape(tokens, step), preferred_element_type=jnp.float32
             )
-            tgb[h, :, at] = (head + scale * tail).astype(jnp.bfloat16)
+            place = pl.ds(pl.multiple_of(h * half + i * step, step), step)
+            tg[:, place] = (head + scale * tail).astype(jnp.bfloat16)
             return carry
 
         lax.fori_loop(0, half // step, table_cols, 0)
-        copy = pltpu.make_async_copy(tgb.at[h], tg.at[:, h * half:(h + 1) * half], tg_s.at[h])
-        copy.start()
-        stores.append(copy)
-
-    table_half(0)
-    mine = pf[2 * x + c]
-    for j in range(1, n_x):
-        u = lax.rem(x + j, n_x)
-        arrived(r2.at[u], b_s.at[0], b_r.at[u])
-        mine = mine + r2[u].astype(jnp.float32)
-    pf[2 * x + c] = mine
-    gb[...] = mine.reshape(n_dp, rows, cols).astype(jnp.bfloat16)
-    for j in range(1, n_dp):
-        k = lax.rem(d + j, n_dp)
-        send(gb.at[k], r3.at[d], c_s.at[j], c_r.at[d], (k, t))
-    table_half(1)
-    out = pf[2 * x + c, pl.ds(pl.multiple_of(d * rows, rows), rows), :]
+
+    out = hg[...]
     for j in range(1, n_dp):
         k = lax.rem(d + j, n_dp)
         arrived(r3.at[k], c_s.at[0], c_r.at[k])
@@ -204,8 +231,6 @@
     hg[...] = out
     for copy in sent:
         copy.wait_send()
-    for copy in stores:
-        copy.wait()
 
 
 def per_device(n_dp, n_t, hidden, tied_table, targets, loss_weight, inputs, embed_grad):
@@ -213,12 +238,6 @@
     vocab = tied_table.shape[0]
     tokens, half, cols, n_x = n_dp * rows, width // 2, width // n_t, n_t // 2
     f32, bf16 = jnp.float32, jnp.bfloat16
-    lane = lax.broadcasted_iota(jnp.int32, (rows, 128), 1)
-    meta = jnp.where(
-        lane == 0,
-        targets.astype(f32)[:, None],
-        jnp.where(lane == 1, inputs.astype(f32)[:, None], loss_weight.astype(f32)[:, None]),
-    )
     vmem = pl.BlockSpec(memory_space=pltpu.VMEM)
     dma = lambda n: pltpu.SemaphoreType.DMA((n,))
     n_a = n_dp // 2
@@ -226,40 +245,42 @@
     return pl.pallas_call(
         functools.partial(kernel, n_dp, n_t, math.sqrt(width)),
         out_shape=(
-            jax.ShapeDtypeStruct((vocab, width), bf16),
-            jax.ShapeDtypeStruct((rows, cols), f32),
+            pltpu.VMEM((vocab, width), bf16),
+            pltpu.VMEM((rows, cols), f32),
         ),
-        in_specs=[vmem, vmem, vmem, pl.BlockSpec(memory_space=pl.ANY)],
-        out_specs=(pl.BlockSpec(memory_space=pl.ANY), vmem),
+        in_specs=[vmem] * 5 + [pl.BlockSpec(memory_space=pl.ANY)],
+        out_specs=(vmem, vmem),
         scratch_shapes=[
             pltpu.VMEM((2, n_dp, rows, half), bf16),
             pltpu.VMEM((2, n_dp, rows, half), bf16),
-            pltpu.VMEM((n_dp, rows, 128), f32),
+            pltpu.VMEM((n_dp, 8, 128), f32),
+            pltpu.VMEM((8, tokens), f32),
             pltpu.VMEM((vocab, width), bf16),
-            pltpu.VMEM((2, vocab, half), bf16),
             pltpu.VMEM((vocab, tokens), f32),
             pltpu.VMEM((vocab, tokens), bf16),
             pltpu.VMEM((vocab, tokens), bf16),
             pltpu.VMEM((tokens, vocab), bf16),
             pltpu.VMEM((n_t, 8, tokens), f32),
             pltpu.VMEM((n_dp, 8, tokens), f32),
-            pltpu.VMEM((n_t, tokens, cols), f32),
-            pltpu.VMEM((n_t, tokens, cols), bf16),
+            pltpu.VMEM((n_t, tokens, cols) if cols % 128 else (8, 128), f32),
+            pltpu.VMEM((n_x, tokens, cols), f32),
             pltpu.VMEM((n_x, tokens, cols), bf16),
             pltpu.VMEM((n_x, tokens, cols), bf16),
-            pltpu.VMEM((n_x, tokens, cols), bf16),
+            pltpu.VMEM((n_x, n_dp, rows, cols), bf16),
+            pltpu.VMEM((n_x, n_dp, rows, cols), bf16),
             pltpu.VMEM((n_dp, rows, cols), bf16),
             pltpu.VMEM((n_dp, rows, cols), bf16),
             *gather_sems, *gather_sems,
             dma(n_a), dma(n_a), dma(n_dp),
             dma(n_t), dma(n_t), dma(n_dp), dma(n_dp),
-            dma(n_x), dma(n_x), dma(n_x), dma(n_x), dma(n_dp), dma(n_dp),
-            pltpu.SemaphoreType.DMA, dma(2),
+            dma(n_x), dma(n_x), pltpu.SemaphoreType.DMA((n_x, 2)), pltpu.SemaphoreType.DMA((n_x, 2)),
+            dma(n_dp), dma(n_dp),
+            pltpu.SemaphoreType.DMA,
         ],
         compiler_params=pltpu.CompilerParams(
             collective_id=0, has_side_effects=True, vmem_limit_bytes=56 << 20
         ),
-    )(hidden, embed_grad, meta, tied_table)
+    )(hidden, embed_grad, targets[None], inputs[None], loss_weight[None], tied_table)
 
 
 def solution(mesh):

time: 55.8 us -> 48.4 us (0.87)
  local copies, waits for them, and re-layouts: 5.49 us -> 2.82 us
  other arithmetic: 2.65 us -> 0 us
  Pallas kernels: 46.8 us -> 44.8 us
    unnamed x4 -> x2, local copies, waits for them, and re-layouts: 5.49 us -> 2.82 us
    pallas_call x1, Pallas kernels: 46.8 us -> 44.8 us  [per_device(): pl.pallas_call(functools.partial(kernel, n_dp, n_t, math.sqrt(width)), ou...]
    convert_element_type x3 -> x0, other arithmetic: 1.97 us -> none  [the longest x1 0.66 us: per_device(): targets.astype(f32)[:, None]]
    select_n x1 -> x0, other arithmetic: 0.67 us -> none  [per_device(): jnp.where(lane == 0, targets.astype(f32)[:, None], jnp.where(lane == 1, i...]
where the time goes in v2:
time: 48.4 us; the launch traced here: 48.3 us
  Pallas kernels  44.8 us (93%)
  local copies, waits for them, and re-layouts  2.82 us (6%)
  between operations  0.64 us (1%)
    pallas_call x1, Pallas kernels, per_device(): pl.pallas_call(functools.partial(kernel, n_dp, n_t, math.sqrt(width)), ou...  44.8 us
    unnamed x2, local copies, waits for them, and re-layouts  2.82 us

profile of v2, /device:TPU:0, one launch (start us, length us, event | category | flops | bytes accessed | tf_op | source)
XLA Modules:
  0.0 48.3 jit_solution(2139178774233621943)
XLA Ops:
  0.6 44.8 %shard_map.77 = (bf16[512,4608]{1,0:T(8,128)(2,1)S(1)}, f32[16,1152]{1,0:T(8,128)S(1)}) custom-call(bf16[16,4608]{1,0:T(8,128)(2,1)} %hid.1, bf16[16,4608]{1,0:T(8,128)(2,1)} %emb.1, s32[1,16]{1,0:T(1,128)} %bitcast.3, s32[1,16]{1,0:T(1,128)} %bitcast.4, bf16[1,16]{1,0:T(2,128)(2,1)} %bitcast.5, bf16[512,4608]{1,0:T(8,128)(2,1)} %table.1), custom_call_target="tpu_custom_call" | custom-call | tf_op jit(solution)/shard_map/pallas_call | solution.py:245
  45.4 2.2 %copy.10 = bf16[512,4608]{1,0:T(8,128)(2,1)} copy(bf16[512,4608]{1,0:T(8,128)(2,1)S(1)} %get-tuple-element.2) | data formatting | bytes 9437184
  47.6 0.6 %copy.11 = f32[16,1152]{1,0:T(8,128)} copy(f32[16,1152]{1,0:T(8,128)S(1)} %get-tuple-element.3) | data formatting | bytes 147456

commit v3 on v2

--- a/solution.py
+++ b/solution.py
@@ -31,6 +31,11 @@
     vocab = tab.shape[0]
     cols = width // n_t
 
+    barrier = pltpu.get_barrier_semaphore()
+    for j in range(1, n_t):
+        pl.semaphore_signal(barrier, inc=1, device_id=(d, lax.rem(t + j, n_t)), device_id_type=MESH)
+    for j in range(1, n_dp):
+        pl.semaphore_signal(barrier, inc=1, device_id=(lax.rem(d + j, n_dp), t), device_id_type=MESH)
     load = pltpu.make_async_copy(table, tab, tab_s)
     load.start()
     for h in range(2):
@@ -41,11 +46,6 @@
     ma[d, 1:2, 0:rows] = inputs[...].astype(jnp.float32)
     ma[d, 2:3, 0:rows] = weights[...].astype(jnp.float32)
 
-    barrier = pltpu.get_barrier_semaphore()
-    for j in range(1, n_t):
-        pl.semaphore_signal(barrier, inc=1, device_id=(d, lax.rem(t + j, n_t)), device_id_type=MESH)
-    for j in range(1, n_dp):
-        pl.semaphore_signal(barrier, inc=1, device_id=(lax.rem(d + j, n_dp), t), device_id_type=MESH)
     pl.semaphore_wait(barrier, n_t + n_dp - 2)
 
     sent = []
@@ -172,7 +172,8 @@
         give, keep = 2 * u + 1 - c, 2 * u + c
         pb[u] = (term(columns(give)) if aligned else terms[give]).astype(jnp.bfloat16)
         send(pb.at[u], r1.at[u], a_s.at[u], a_r.at[u], (d, sib))
-        pf[u] = term(columns(keep)) if aligned else terms[keep]
+        if j:
+            pf[u] = term(columns(keep)) if aligned else terms[keep]
 
     n_q = 2
     slots = n_dp // n_q
@@ -184,14 +185,35 @@
 
     for j in order:
         u = lax.rem(x + j, n_x)
-        arrived(r1.at[u], a_s.at[0], a_r.at[u])
         if j:
+            arrived(r1.at[u], a_s.at[0], a_r.at[u])
             for q in range(n_q):
                 for i in range(q * slots, (q + 1) * slots):
                     qb[u, i] = pair(u, i).astype(jnp.bfloat16)
                 span = pl.ds(q * slots, slots)
                 send(qb.at[u, span], r2.at[x, span], b_s.at[j, q], b_r.at[x, q], (d, u * 2 + c))
+    arrived(r1.at[x], a_s.at[0], a_r.at[x])
+    pf[x] = term(columns(2 * x + c)) if aligned else terms[2 * x + c]
     gather_side(ea, e_z, e_s, e_r, e_r2)
+    step = 256
+
+    def table_half(h):
+        def table_cols(i, carry):
+            at = pl.ds(pl.multiple_of(i * step, step), step)
+            head = jnp.dot(
+                dl[...], ha[h, :, :, at].reshape(tokens, step), preferred_element_type=jnp.float32
+            )
+            tail = jnp.dot(
+                oh[...], ea[h, :, :, at].reshape(tokens, step), preferred_element_type=jnp.float32
+            )
+            place = pl.ds(pl.multiple_of(h * half + i * step, step), step)
+            tg[:, place] = (head + scale * tail).astype(jnp.bfloat16)
+            return carry
+
+        lax.fori_loop(0, half // step, table_cols, 0)
+
+    gather_end(ea, e_z, e_r2)
+    table_half(0)
     for q in range(n_q):
         for j in range(1, n_x):
             u = lax.rem(x + j, n_x)
@@ -205,24 +227,8 @@
                 send(gb.at[i], r3.at[d], c_s.at[i], c_r.at[d], (lax.rem(d + 1 + i, n_dp), t))
             else:
                 hg[...] = mine
-    gather_end(ea, e_z, e_r2)
-
-    step = 256
-    for h in range(2):
-        def table_cols(i, carry):
-            at = pl.ds(pl.multiple_of(i * step, step), step)
-            head = jnp.dot(
-                dl[...], ha[h, :, :, at].reshape(tokens, step), preferred_element_type=jnp.float32
-            )
-            tail = jnp.dot(
-                oh[...], ea[h, :, :, at].reshape(tokens, step), preferred_element_type=jnp.float32
-            )
-            place = pl.ds(pl.multiple_of(h * half + i * step, step), step)
-            tg[:, place] = (head + scale * tail).astype(jnp.bfloat16)
-            return carry
-
-        lax.fori_loop(0, half // step, table_cols, 0)
-
+
+    table_half(1)
     out = hg[...]
     for j in range(1, n_dp):
         k = lax.rem(d + j, n_dp)

time: 48.4 us -> 46.7 us (0.965)
  Pallas kernels: 44.8 us -> 43.1 us
    pallas_call x1, Pallas kernels: 44.8 us -> 43.1 us  [per_device(): pl.pallas_call(functools.partial(kernel, n_dp, n_t, math.sqrt(width)), ou...]
where the time goes in v3:
time: 46.7 us; the launch traced here: 46.6 us
  Pallas kernels  43.1 us (92%)
  local copies, waits for them, and re-layouts  2.82 us (6%)
  between operations  0.64 us (1%)
    pallas_call x1, Pallas kernels, per_device(): pl.pallas_call(functools.partial(kernel, n_dp, n_t, math.sqrt(width)), ou...  43.1 us
    unnamed x2, local copies, waits for them, and re-layouts  2.82 us

profile of v3, /device:TPU:0, one launch (start us, length us, event | category | flops | bytes accessed | tf_op | source)
XLA Modules:
  0.0 46.6 jit_solution(1500556604914183718)
XLA Ops:
  0.6 43.1 %shard_map.77 = (bf16[512,4608]{1,0:T(8,128)(2,1)S(1)}, f32[16,1152]{1,0:T(8,128)S(1)}) custom-call(bf16[16,4608]{1,0:T(8,128)(2,1)} %hid.1, bf16[16,4608]{1,0:T(8,128)(2,1)} %emb.1, s32[1,16]{1,0:T(1,128)} %bitcast.3, s32[1,16]{1,0:T(1,128)} %bitcast.4, bf16[1,16]{1,0:T(2,128)(2,1)} %bitcast.5, bf16[512,4608]{1,0:T(8,128)(2,1)} %table.1), custom_call_target="tpu_custom_call" | custom-call | tf_op jit(solution)/shard_map/pallas_call | solution.py:251
  43.8 2.2 %copy.10 = bf16[512,4608]{1,0:T(8,128)(2,1)} copy(bf16[512,4608]{1,0:T(8,128)(2,1)S(1)} %get-tuple-element.2) | data formatting | bytes 9437184
  45.9 0.6 %copy.11 = f32[16,1152]{1,0:T(8,128)} copy(f32[16,1152]{1,0:T(8,128)S(1)} %get-tuple-element.3) | data formatting | bytes 147456

commit v4 on v3

--- a/solution.py
+++ b/solution.py
@@ -91,16 +91,37 @@
             k = lax.rem(d + j, n_dp)
             arrived(buf.at[1 - c, k], z.at[0], r2.at[k])
 
+    e = lax.rem(x, 2)
+    across = (x + 1 - 2 * e) * 2 + c
+    quarter = half // 2
+
+    def cut(k, part):
+        return ha.at[c, k, :, pl.ds(pl.multiple_of(part * quarter, 128), quarter)]
+
+    for j in range(1, n_a):
+        send(cut(d, e), cut(d, e), h_z.at[j], h_r.at[d], (up(j), t))
+    send(ha.at[c, d], ha.at[c, d], h_y.at[0], h_r.at[d], (side, t))
+    for j in range(1, n_a):
+        k = down(j) + b
+        arrived(cut(k, e), h_z.at[0], h_r.at[k])
+        send(cut(k, e), cut(k, e), h_z.at[n_a + j], h_r.at[n_dp + k], (d, across))
+        send(cut(k, e), cut(k, e), h_y.at[j], h_r.at[k], (side, t))
+    for j in range(1, n_a):
+        k = down(j) + b
+        arrived(cut(k, 1 - e), h_z.at[0], h_r.at[n_dp + k])
+        send(cut(k, 1 - e), cut(k, 1 - e), h_y.at[n_a + j], h_r.at[n_dp + k], (side, t))
+        send(ha.at[c, k], ha.at[c, k], h_s.at[k], h_r2.at[k], (d, sib))
+    for j in range(n_a):
+        k = down(j) + 1 - b
+        if j:
+            arrived(cut(k, e), h_z.at[0], h_r.at[k])
+            arrived(cut(k, 1 - e), h_z.at[0], h_r.at[n_dp + k])
+        else:
+            arrived(ha.at[c, k], h_z.at[0], h_r.at[k])
+        send(ha.at[c, k], ha.at[c, k], h_s.at[k], h_r2.at[k], (d, sib))
     for j in range(1, n_a):
         send(ma.at[d], ma.at[d], m_z.at[j], m_r.at[d], (up(j), t))
     send(ma.at[d], ma.at[d], m_y.at[0], m_r.at[d], (side, t))
-    gather_start(ha, h_z, h_y, h_r)
-    gather_far(ha, h_z, h_y, h_s, h_r, h_r2)
-    for j in range(1, n_a):
-        k = down(j) + b
-        arrived(ma.at[k], m_z.at[0], m_r.at[k])
-        send(ma.at[k], ma.at[k], m_y.at[j], m_r.at[k], (side, t))
-    gather_side(ha, h_z, h_s, h_r, h_r2)
     gather_start(ea, e_z, e_y, e_r)
     load.wait()
     piece = min(vocab, 256)
@@ -131,9 +152,9 @@
     for j in range(1, n_t):
         send(sa.at[t], sa.at[t], sa_s.at[j], sa_r.at[t], (d, lax.rem(t + j, n_t)))
     for j in range(1, n_a):
-        k = down(j) + 1 - b
+        k = down(j) + b
         arrived(ma.at[k], m_z.at[0], m_r.at[k])
-    arrived(ma.at[side], m_z.at[0], m_r.at[side])
+        send(ma.at[k], ma.at[k], m_y.at[j], m_r.at[k], (side, t))
     for j in range(1, n_t):
         k = lax.rem(t + j, n_t)
         arrived(sa.at[k], sa_s.at[0], sa_r.at[k])
@@ -141,6 +162,10 @@
     for j in range(1, n_dp):
         send(sd.at[d], sd.at[d], sd_s.at[j], sd_r.at[d], (lax.rem(d + j, n_dp), t))
     gather_far(ea, e_z, e_y, e_s, e_r, e_r2)
+    for j in range(1, n_a):
+        k = down(j) + 1 - b
+        arrived(ma.at[k], m_z.at[0], m_r.at[k])
+    arrived(ma.at[side], m_z.at[0], m_r.at[side])
     for k in range(n_dp):
         ids[:, k * rows:(k + 1) * rows] = ma[k, :, 0:rows]
     base = (d * n_t + t) * vocab
@@ -276,7 +301,7 @@
             pltpu.VMEM((n_x, n_dp, rows, cols), bf16),
             pltpu.VMEM((n_dp, rows, cols), bf16),
             pltpu.VMEM((n_dp, rows, cols), bf16),
-            *gather_sems, *gather_sems,
+            dma(2 * n_a), dma(2 * n_a), dma(n_dp), dma(2 * n_dp), dma(n_dp), *gather_sems,
             dma(n_a), dma(n_a), dma(n_dp),
             dma(n_t), dma(n_t), dma(n_dp), dma(n_dp),
             dma(n_x), dma(n_x), pltpu.SemaphoreType.DMA((n_x, 2)), pltpu.SemaphoreType.DMA((n_x, 2)),

time: 46.7 us -> 46.2 us (0.989)
  Pallas kernels: 43.1 us -> 42.6 us
    pallas_call x1, Pallas kernels: 43.1 us -> 42.6 us  [per_device(): pl.pallas_call(functools.partial(kernel, n_dp, n_t, math.sqrt(width)), ou...]
where the time goes in v4:
time: 46.2 us; the launch traced here: 46.1 us
  Pallas kernels  42.6 us (92%)
  local copies, waits for them, and re-layouts  2.82 us (6%)
  between operations  0.64 us (1%)
    pallas_call x1, Pallas kernels, per_device(): pl.pallas_call(functools.partial(kernel, n_dp, n_t, math.sqrt(width)), ou...  42.6 us
    unnamed x2, local copies, waits for them, and re-layouts  2.82 us

profile of v4, /device:TPU:0, one launch (start us, length us, event | category | flops | bytes accessed | tf_op | source)
XLA Modules:
  0.0 46.1 jit_solution(12698516572937816652)
XLA Ops:
  0.6 42.6 %shard_map.77 = (bf16[512,4608]{1,0:T(8,128)(2,1)S(1)}, f32[16,1152]{1,0:T(8,128)S(1)}) custom-call(bf16[16,4608]{1,0:T(8,128)(2,1)} %hid.1, bf16[16,4608]{1,0:T(8,128)(2,1)} %emb.1, s32[1,16]{1,0:T(1,128)} %bitcast.3, s32[1,16]{1,0:T(1,128)} %bitcast.4, bf16[1,16]{1,0:T(2,128)(2,1)} %bitcast.5, bf16[512,4608]{1,0:T(8,128)(2,1)} %table.1), custom_call_target="tpu_custom_call" | custom-call | tf_op jit(solution)/shard_map/pallas_call | solution.py:276
  43.2 2.2 %copy.10 = bf16[512,4608]{1,0:T(8,128)(2,1)} copy(bf16[512,4608]{1,0:T(8,128)(2,1)S(1)} %get-tuple-element.2) | data formatting | bytes 9437184
  45.4 0.6 %copy.11 = f32[16,1152]{1,0:T(8,128)} copy(f32[16,1152]{1,0:T(8,128)S(1)} %get-tuple-element.3) | data formatting | bytes 147456

commit v5 on v4

--- a/solution.py
+++ b/solution.py
@@ -200,7 +200,7 @@
         if j:
             pf[u] = term(columns(keep)) if aligned else terms[keep]
 
-    n_q = 2
+    n_q = 4
     slots = n_dp // n_q
 
     def pair(u, i):
@@ -304,7 +304,7 @@
             dma(2 * n_a), dma(2 * n_a), dma(n_dp), dma(2 * n_dp), dma(n_dp), *gather_sems,
             dma(n_a), dma(n_a), dma(n_dp),
             dma(n_t), dma(n_t), dma(n_dp), dma(n_dp),
-            dma(n_x), dma(n_x), pltpu.SemaphoreType.DMA((n_x, 2)), pltpu.SemaphoreType.DMA((n_x, 2)),
+            dma(n_x), dma(n_x), pltpu.SemaphoreType.DMA((n_x, 4)), pltpu.SemaphoreType.DMA((n_x, 4)),
             dma(n_dp), dma(n_dp),
             pltpu.SemaphoreType.DMA,
         ],

time: 46.2 us -> 45.8 us (level)
  Pallas kernels: 42.6 us -> 42.1 us
where the time goes in v5:
time: 45.8 us; the launch traced here: 45.6 us
  Pallas kernels  42.1 us (92%)
  local copies, waits for them, and re-layouts  2.82 us (6%)
  between operations  0.64 us (1%)
    pallas_call x1, Pallas kernels, per_device(): pl.pallas_call(functools.partial(kernel, n_dp, n_t, math.sqrt(width)), ou...  42.1 us
    unnamed x2, local copies, waits for them, and re-layouts  2.82 us

profile of v5, /device:TPU:0, one launch (start us, length us, event | category | flops | bytes accessed | tf_op | source)
XLA Modules:
  0.0 45.6 jit_solution(6413505498178018604)
XLA Ops:
  0.6 42.1 %shard_map.77 = (bf16[512,4608]{1,0:T(8,128)(2,1)S(1)}, f32[16,1152]{1,0:T(8,128)S(1)}) custom-call(bf16[16,4608]{1,0:T(8,128)(2,1)} %hid.1, bf16[16,4608]{1,0:T(8,128)(2,1)} %emb.1, s32[1,16]{1,0:T(1,128)} %bitcast.3, s32[1,16]{1,0:T(1,128)} %bitcast.4, bf16[1,16]{1,0:T(2,128)(2,1)} %bitcast.5, bf16[512,4608]{1,0:T(8,128)(2,1)} %table.1), custom_call_target="tpu_custom_call" | custom-call | tf_op jit(solution)/shard_map/pallas_call | solution.py:276
  42.8 2.2 %copy.10 = bf16[512,4608]{1,0:T(8,128)(2,1)} copy(bf16[512,4608]{1,0:T(8,128)(2,1)S(1)} %get-tuple-element.2) | data formatting | bytes 9437184
  45.0 0.6 %copy.11 = f32[16,1152]{1,0:T(8,128)} copy(f32[16,1152]{1,0:T(8,128)S(1)} %get-tuple-element.3) | data formatting | bytes 147456
